TPU v7x, 256 devices: a whole 4x4x8 slice. The times are simulated.
256 devices in a mesh: strip: 16 (over z_lo, y, core), tensor: 16 (over x, z_hi).
Axes of the slice: x: 4, y: 4, z: 8 (z_hi: 4, z_lo: 2; z = z_hi * 2 + z_lo), core: 2. Of those that a mesh axis runs over, the one named last changes fastest.
Arguments:
- conv_out: bfloat16 [128, 256, 1536], P('strip', 'tensor'), may hold values from -425 to 425
- out_grad: bfloat16 [128, 256, 1536], P('strip', 'tensor'), may hold values from -6 to 6
- layer_norm_gain: float32 [1536], replicated, may hold values from 0.5 to 2
- layer_norm_bias: float32 [1536], replicated, may hold values from -3 to 3
- w_in: bfloat16 [1536, 6144], P('strip', 'tensor'), may hold values from -0.15625 to 0.15625
- b_in: float32 [6144], P('tensor'), may hold values from -3 to 3
- w_out: bfloat16 [6144, 1536], P('tensor', 'strip'), may hold values from -0.078125 to 0.078125
- layer_scale: float32 [1536], replicated, may hold values from 0.25 to 2
- dw_kernel: float32 [7, 7, 1536], replicated, may hold values from -0.875 to 0.875
Outputs:
- grad_input: bfloat16 [128, 256, 1536], P('strip', 'tensor')
- grad_w_in: float32 [1536, 6144], P('strip', 'tensor')
- grad_w_out: float32 [6144, 1536], P('tensor', 'strip')
All inputs are finite; a program needn't handle non-finite values.
Results may differ from a plain program's by a relative error of at most 0.0063.
Values may be sent and summed in bfloat16 or wider, within the bound.
No kernel may reach another device: no remote copies, remote signals or barrier semaphores. Data moves between devices by JAX's collectives and lax.ppermute only.
A program may use at most 128 MiB of HBM per device.

v0:
```python
import math
import jax
import jax.numpy as jnp
from jax import lax
from jax.sharding import PartitionSpec as P

ln_eps = 1e-06
root_half = 0.7071067811865476
density_norm = 0.3989422804014327


def with_halo(block, sides, width):
    for axis, dim in sides:
        count = lax.axis_size(axis)
        forward = [(i, i + 1) for i in range(count - 1)]
        backward = [(target, source) for source, target in forward]
        low = lax.ppermute(
            lax.slice_in_dim(block, block.shape[dim] - width, None, axis=dim), axis, forward
        )
        high = lax.ppermute(lax.slice_in_dim(block, 0, width, axis=dim), axis, backward)
        block = jnp.concatenate([low, block, high], axis=dim)
    return block


def gelu_value(value):
    return 0.5 * value * (1.0 + lax.erf(value * root_half))


def gelu_slope(value):
    return (
        0.5 * (1.0 + lax.erf(value * root_half))
        + value * jnp.exp(-0.5 * value * value) * density_norm
    )


def apply_layer_norm(flattened_rows):
    centre = jnp.mean(flattened_rows, axis=-1, keepdims=True)
    centred = flattened_rows - centre
    spread = jnp.mean(centred * centred, axis=-1, keepdims=True)
    inverse_deviation = lax.rsqrt(spread + ln_eps)
    return (centred * inverse_deviation, inverse_deviation)


def layer_norm_backward(normed_gradient, centred_input, inverse_deviation, layer_norm_gain):
    gain_scaled = normed_gradient * layer_norm_gain
    first_moment = jnp.mean(gain_scaled, axis=-1, keepdims=True)
    second_moment = jnp.mean(gain_scaled * centred_input, axis=-1, keepdims=True)
    return inverse_deviation * (gain_scaled - first_moment - centred_input * second_moment)


def transpose_conv(padded, dw_kernel, image_height, image_breadth):
    taps = dw_kernel.shape[0]
    total = jnp.zeros((image_height, image_breadth, padded.shape[2]), jnp.float32)
    for row_tap in range(taps):
        for col_tap in range(taps):
            start_row = taps - 1 - row_tap
            start_col = taps - 1 - col_tap
            total = (
                total
                + dw_kernel[row_tap, col_tap]
                * padded[
                    start_row : start_row + image_height, start_col : start_col + image_breadth
                ]
            )
    return total


def body(
    conv_out, out_grad, layer_norm_gain, layer_norm_bias, w_in, b_in, w_out, layer_scale, dw_kernel
):
    tile_rows, tile_cols, channel_count = conv_out.shape
    local_count = tile_rows * tile_cols
    flattened_rows = conv_out.astype(jnp.float32).reshape(local_count, channel_count)
    centred_input, inverse_deviation = apply_layer_norm(flattened_rows)
    normed_output = (centred_input * layer_norm_gain + layer_norm_bias).astype(jnp.bfloat16)
    upstream = out_grad.astype(jnp.float32)
    scaled_grad = (upstream.reshape(local_count, channel_count) * layer_scale).astype(jnp.bfloat16)
    w_in_part, w_out_part = (
        lax.all_gather(w_in, "strip", axis=0, tiled=True),
        lax.all_gather(w_out, "strip", axis=1, tiled=True),
    )
    normed_all, scaled_all = (
        lax.all_gather(normed_output, "tensor", axis=0, tiled=True),
        lax.all_gather(scaled_grad, "tensor", axis=0, tiled=True),
    )
    pre_act = jnp.dot(normed_all, w_in_part, preferred_element_type=jnp.float32) + b_in
    hidden_act = gelu_value(pre_act).astype(jnp.bfloat16)
    back_act = lax.dot_general(
        scaled_all, w_out_part, (((1,), (1,)), ((), ())), preferred_element_type=jnp.float32
    )
    back_pre = (back_act * gelu_slope(pre_act)).astype(jnp.bfloat16)
    grad_in = lax.dot_general(
        normed_all, back_pre, (((0,), (0,)), ((), ())), preferred_element_type=jnp.float32
    )
    grad_out = lax.dot_general(
        hidden_act, scaled_all, (((0,), (0,)), ((), ())), preferred_element_type=jnp.float32
    )
    normed_gradient = lax.psum_scatter(
        lax.dot_general(
            back_pre, w_in_part, (((1,), (1,)), ((), ())), preferred_element_type=jnp.float32
        ).astype(jnp.bfloat16),
        "tensor",
        scatter_dimension=0,
        tiled=True,
    ).astype(jnp.float32)
    summed_in, summed_out = (
        lax.psum_scatter(grad_in, "strip", scatter_dimension=0, tiled=True),
        lax.psum_scatter(grad_out, "strip", scatter_dimension=1, tiled=True),
    )
    total_tokens = local_count * lax.axis_size("strip") * lax.axis_size("tensor")
    factor = 1.0 / math.sqrt(total_tokens)
    convolution_gradient = (
        layer_norm_backward(normed_gradient, centred_input, inverse_deviation, layer_norm_gain)
        .astype(jnp.bfloat16)
        .reshape(tile_rows, tile_cols, channel_count)
    )
    margin = dw_kernel.shape[0] // 2
    padded = with_halo(convolution_gradient, (("strip", 0), ("tensor", 1)), margin)
    grad_input = (
        upstream + transpose_conv(padded.astype(jnp.float32), dw_kernel, tile_rows, tile_cols)
    ).astype(jnp.bfloat16)
    return (grad_input, summed_in * factor, summed_out * factor)


def solution(mesh):
    return jax.shard_map(
        body,
        mesh=mesh,
        in_specs=(
            P("strip", "tensor", None),
            P("strip", "tensor", None),
            P(),
            P(),
            P("strip", "tensor"),
            P("tensor"),
            P("tensor", "strip"),
            P(),
            P(),
        ),
        out_specs=(P("strip", "tensor", None), P("strip", "tensor"), P("tensor", "strip")),
        check_vma=False,
    )
```

profile of v0, /device:TPU:2, one launch (start us, length us, event | category | flops | bytes accessed | tf_op | source)
XLA Modules:
  0.0 560.2 jit_solution(12956353183333648456)
XLA Ops:
  7.2 0.0 all-gather.11.cloned.1.call-start
  7.2 0.7 all-gather.11.cloned.1.call-update
  7.9 0.0 all-gather.9.cloned.1.call-start
  8.0 1.1 convert_reduce_fusion
  9.1 0.1 div.16
  9.2 1.2 multiply_reduce_fusion.1
  10.4 0.1 rsqrt.12
  10.5 2.1 add_convert_fusion
  12.6 0.0 all-gather.9.cloned.1.call-update
  12.6 0.0 all-gather.7.cloned.1.call-start
  12.7 0.7 all-gather.7.cloned.1.call-update
  13.3 0.0 all-gather.5.cloned.1.call-start
  13.4 1.8 fusion.59
  15.2 0.0 all-gather.5.cloned.1.call-update
  15.2 0.0 reduce-scatter.4.cloned.1.call-start
  15.3 32.9 %all-gather.11.cloned.1.call-done = bf16[1536,384]{1,0:T(8,128)(2,1)} async-done(((bf16[96,384]{1,0:T(8,128)(2,1)}), bf16[1536,384]{1,0:T(8,128)(2,1)}) %all-gather.11.cloned.1.call-update) | async-done | bytes 1179664 | tf_op jit(solution)/shard_map/all_gather | solution.py:79
  48.2 100.3 %all-gather.9.cloned.1.call-done = bf16[2048,1536]{1,0:T(8,128)(2,1)} async-done(((bf16[128,1536]{1,0:T(8,128)(2,1)}), bf16[2048,1536]{1,0:T(8,128)(2,1)}) %all-gather.9.cloned.1.call-update) | async-done | bytes 6291472 | tf_op jit(solution)/shard_map/all_gather | solution.py:83
  148.5 8.2 %convolution_add_fusion = f32[2048,384]{1,0:T(8,128)} fusion(bf16[2048,1536]{1,0:T(8,128)(2,1)} %all-gather.9.cloned.1.call-done, bf16[1536,384]{1,0:T(8,128)(2,1)} %all-gather.11.cloned.1.call-done, f32[384]{0:T(512)S(1)} %copy-done.5), kind=kOutput, calls=%fused_computation.10 | convolution fusion | flops 2416705536 | bytes 10618368 | tf_op jit(solution)/shard_map/dot_general | solution.py:86
  156.7 27.4 %all-gather.7.cloned.1.call-done = bf16[384,1536]{0,1:T(8,128)(2,1)} async-done(((bf16[384,96]{0,1:T(8,128)(2,1)}), bf16[384,1536]{0,1:T(8,128)(2,1)}) %all-gather.7.cloned.1.call-update) | async-done | bytes 1179664 | tf_op jit(solution)/shard_map/all_gather | solution.py:80
  184.1 99.5 %all-gather.5.cloned.1.call-done = bf16[2048,1536]{1,0:T(8,128)(2,1)} async-done(((bf16[128,1536]{1,0:T(8,128)(2,1)}), bf16[2048,1536]{1,0:T(8,128)(2,1)}) %all-gather.5.cloned.1.call-update) | async-done | bytes 6291472 | tf_op jit(solution)/shard_map/all_gather | solution.py:84
  283.6 8.3 %fusion.5 = bf16[2048,384]{1,0:T(8,128)(2,1)S(1)} fusion(f32[2048,384]{1,0:T(8,128)} %convolution_add_fusion, bf16[2048,1536]{1,0:T(8,128)(2,1)} %all-gather.5.cloned.1.call-done, bf16[384,1536]{0,1:T(8,128)(2,1)} %all-gather.7.cloned.1.call-done), kind=kOutput, calls=%fused_computation.7 | convolution fusion | flops 2423783424 | bytes 12189696 | tf_op jit(solution)/shard_map/dot_general | solution.py:88
  291.9 1.2 copy-done.6
  293.1 5.4 convolution_convert_fusion
  298.5 0.0 reduce-scatter.4.cloned.1.call-update
  298.6 0.2 reduce-scatter.6.cloned.1.call-start
  298.8 1.2 copy-done.7
  300.0 7.7 %fusion.63 = f32[1536,384]{1,0:T(8,128)} fusion(bf16[2048,1536]{1,0:T(8,128)(2,1)} %all-gather.9.cloned.1.call-done, bf16[2048,384]{1,0:T(8,128)(2,1)S(1)} %copy-done.7), kind=kOutput, calls=%fused_computation.184 | convolution fusion | flops 2415919104 | bytes 10223616 | tf_op jit(solution)/shard_map/dot_general | solution.py:92
  307.6 0.0 reduce-scatter.6.cloned.1.call-update
  307.7 0.0 reduce-scatter.8.cloned.1.call-start
  307.7 9.0 %fusion.6 = f32[384,1536]{0,1:T(8,128)} fusion(bf16[2048,1536]{1,0:T(8,128)(2,1)} %all-gather.5.cloned.1.call-done, f32[2048,384]{1,0:T(8,128)} %convolution_add_fusion), kind=kOutput, calls=%fused_computation.11 | convolution fusion | flops 2419851264 | bytes 11796480 | tf_op jit(solution)/shard_map/dot_general | solution.py:95
  316.7 0.0 reduce-scatter.8.cloned.1.call-update
  316.8 0.8 slice_reduce_fusion.46
  317.6 0.9 slice_reduce_fusion.48
  318.5 0.9 slice_reduce_fusion.47
  319.4 86.1 %reduce-scatter.4.cloned.1.call-done = bf16[128,1536]{1,0:T(8,128)(2,1)} async-done(((bf16[2048,1536]{1,0:T(8,128)(2,1)}), bf16[128,1536]{1,0:T(8,128)(2,1)}) %reduce-scatter.4.cloned.1.call-update) | async-done | bytes 393232 | tf_op jit(solution)/shard_map/reduce_scatter | solution.py:98
  405.5 1.3 fusion.60
  406.8 1.4 multiply_convert_fusion.2
  408.2 1.3 collective-permute-start.1
  409.5 3.0 collective-permute-start
  412.6 61.1 %reduce-scatter.6.cloned.1.call-done = f32[96,384]{1,0:T(8,128)} async-done(((f32[1536,384]{1,0:T(8,128)}), f32[96,384]{1,0:T(8,128)}) %reduce-scatter.6.cloned.1.call-update) | async-done | bytes 147472 | tf_op jit(solution)/shard_map/reduce_scatter | solution.py:107
  473.7 1.6 broadcast_multiply_fusion.1
  475.3 0.1 pad_maximum_fusion.2
  475.4 4.4 collective-permute-start.2
  479.9 4.4 collective-permute-start.3
  484.3 59.4 %reduce-scatter.8.cloned.1.call-done = f32[384,96]{0,1:T(8,128)} async-done(((f32[384,1536]{0,1:T(8,128)}), f32[384,96]{0,1:T(8,128)}) %reduce-scatter.8.cloned.1.call-update) | async-done | bytes 147472 | tf_op jit(solution)/shard_map/reduce_scatter | solution.py:108
  543.6 1.6 broadcast_multiply_fusion
  545.2 0.4 maximum_convert_fusion
  545.6 7.7 %fusion.10 = bf16[8,16,1536]{2,1,0:T(8,128)(2,1)} fusion(f32[14,22,1536]{2,1,0:T(8,128)S(1)} %maximum_convert_fusion, f32[1536]{0:T(1024)} %get-tuple-element.52, f32[1536]{0:T(1024)} %get-tuple-element.53, f32[1536]{0:T(1024)} %get-tuple-element.6, f32[1536]{0:T(1024)} %get-tuple-element.7, f32[1536]{0:T(1024)} %get-tuple-element.8, ...), kind=kLoop, calls=%fused_computation.17 | loop fusion | flops 19660800 | bytes 39622656 | tf_op jit(solution)/shard_map/convert_element_type | solution.py:121
  (22 shorter events, 0.1 us)
Async XLA Ops:
  7.2 141.3 %copy-start.5 = (f32[384]{0:T(512)S(1)}, f32[384]{0:T(512)}, u32[]{:S(2)}) copy-start(f32[384]{0:T(512)} %param.14) | copy-start | bytes 4612
  7.2 41.0 %all-gather.11.cloned.1.call-start = ((), (), s32[]{:S(2)}) async-start(), calls=%async_computation.6 | async-start | bytes 1253376 | tf_op jit(solution)/shard_map/all_gather | solution.py:79
  7.9 140.5 %all-gather.9.cloned.1.call-start = ((), (), s32[]{:S(2)}) async-start(), calls=%async_computation.5 | async-start | bytes 6684672 | tf_op jit(solution)/shard_map/all_gather | solution.py:83
  12.6 171.5 %all-gather.7.cloned.1.call-start = ((), (), s32[]{:S(2)}) async-start(), calls=%async_computation.4 | async-start | bytes 1253376 | tf_op jit(solution)/shard_map/all_gather | solution.py:80
  13.3 270.3 %all-gather.5.cloned.1.call-start = ((), (), s32[]{:S(2)}) async-start(), calls=%async_computation.3 | async-start | bytes 6684672 | tf_op jit(solution)/shard_map/all_gather | solution.py:84
  15.2 390.2 %reduce-scatter.4.cloned.1.call-start = ((), (), s32[]{:S(2)}) async-start(), calls=%async_computation.7 | async-start | bytes 6684672 | tf_op jit(solution)/shard_map/reduce_scatter | solution.py:98
  156.7 136.5 %copy-start.4 = (bf16[1536,384]{1,0:T(8,128)(2,1)S(1)}, bf16[1536,384]{1,0:T(8,128)(2,1)}, u32[]{:S(2)}) copy-start(bf16[1536,384]{1,0:T(8,128)(2,1)} %all-gather.11.cloned.1.call-done) | copy-start | bytes 3538948
  291.9 1.2 copy-start.6
  298.5 1.4 copy-start.7
  298.6 175.1 %reduce-scatter.6.cloned.1.call-start = ((), (), s32[]{:S(2)}) async-start(), calls=%async_computation.8 | async-start | bytes 2506752 | tf_op jit(solution)/shard_map/reduce_scatter | solution.py:107
  307.7 9.1 %copy-start.2 = (f32[7,7,1536]{2,1,0:T(8,128)S(1)}, f32[7,7,1536]{2,1,0:T(8,128)}, u32[]{:S(2)}) copy-start(f32[7,7,1536]{2,1,0:T(8,128)} %param.17) | copy-start | bytes 903172
  307.7 97.8 %copy-start.3 = (f32[1536]{0:T(1024)S(1)}, f32[1536]{0:T(1024)}, u32[]{:S(2)}) copy-start(f32[1536]{0:T(1024)} %param.11) | copy-start | bytes 18436
  307.7 235.9 %reduce-scatter.8.cloned.1.call-start = ((), (), s32[]{:S(2)}) async-start(), calls=%async_computation.9 | async-start | bytes 2506752 | tf_op jit(solution)/shard_map/reduce_scatter | solution.py:108
  316.7 88.7 %copy-start = (bf16[8,16,1536]{2,1,0:T(8,128)(2,1)S(1)}, bf16[8,16,1536]{2,1,0:T(8,128)(2,1)}, u32[]{:S(2)}) copy-start(bf16[8,16,1536]{2,1,0:T(8,128)(2,1)} %param.9) | copy-start | bytes 1179652
  406.8 138.9 %copy-start.1 = (bf16[8,16,1536]{2,1,0:T(8,128)(2,1)S(1)}, bf16[8,16,1536]{2,1,0:T(8,128)(2,1)}, u32[]{:S(2)}) copy-start(bf16[8,16,1536]{2,1,0:T(8,128)(2,1)} %param.10) | copy-start | bytes 1179652
  408.2 67.1 %collective-permute-start.1 = (bf16[3,16,1536]{2,1,0:T(8,128)(2,1)S(1)}, bf16[3,16,1536]{2,1,0:T(8,128)(2,1)S(1)}, u32[]{:S(2)}, u32[]{:S(2)}) collective-permute-start(bf16[3,16,1536]{2,1,0:T(8,128)(2,1)S(1)} %bitcast.29), channel_id=1, source_target_pairs={{16,0},{32,16},{48,32},{64,48},{80,64},{96,80},{112,96},{128,112},... | collective-permute-start | bytes 442376 | tf_op jit(solution)/shard_map/ppermute | solution.py:20
  409.5 65.8 %collective-permute-start = (bf16[3,16,1536]{2,1,0:T(8,128)(2,1)S(1)}, bf16[3,16,1536]{2,1,0:T(8,128)(2,1)S(1)}, u32[]{:S(2)}, u32[]{:S(2)}) collective-permute-start(bf16[3,16,1536]{2,1,0:T(8,128)(2,1)S(1)} %bitcast.28), channel_id=1, source_target_pairs={{0,16},{16,32},{32,48},{48,64},{64,80},{80,96},{96,112},{112,128},... | collective-permute-start | bytes 442376 | tf_op jit(solution)/shard_map/ppermute | solution.py:17
  475.4 69.8 %collective-permute-start.2 = (bf16[14,3,1536]{2,1,0:T(4,128)(2,1)S(1)}, bf16[14,3,1536]{2,1,0:T(4,128)(2,1)S(1)}, u32[]{:S(2)}, u32[]{:S(2)}) collective-permute-start(bf16[14,3,1536]{2,1,0:T(4,128)(2,1)S(1)} %get-tuple-element.54), channel_id=1, source_target_pairs={{0,1},{1,2},{2,3},{3,4},{4,5},{5,6},{6,7},{7,8},{8,9},{9,10},{10,1... | collective-permute-start | bytes 387080 | tf_op jit(solution)/shard_map/ppermute | solution.py:17
  479.9 65.4 %collective-permute-start.3 = (bf16[14,3,1536]{2,1,0:T(4,128)(2,1)S(1)}, bf16[14,3,1536]{2,1,0:T(4,128)(2,1)S(1)}, u32[]{:S(2)}, u32[]{:S(2)}) collective-permute-start(bf16[14,3,1536]{2,1,0:T(4,128)(2,1)S(1)} %get-tuple-element.55), channel_id=1, source_target_pairs={{1,0},{2,1},{3,2},{4,3},{5,4},{6,5},{7,6},{8,7},{9,8},{10,9},{11,1... | collective-permute-start | bytes 387080 | tf_op jit(solution)/shard_map/ppermute | solution.py:20
Sparse Core Ops, SparseCore 0:
  9.9 38.2 all-gather.10
  51.2 97.1 all-gather.8
  150.3 33.7 all-gather.6
  186.4 97.1 all-gather.4
  298.7 106.7 reduce-scatter.3
  407.9 65.7 reduce-scatter.5
  476.2 67.3 reduce-scatter.7
where the time goes:
time: 561 us; the launch traced here: 560 us
  waiting for transfers between devices  468 us (83%)
  matrix products  38.6 us (7%)
  other arithmetic  20.3 us (4%)
  between operations  14.3 us (3%)
  starting transfers between devices  13.6 us (2%)
    all_gather x1, waiting for transfers between devices, body(): lax.all_gather(normed_output, 'tensor', axis=0, tiled=True)  100 us
    all_gather x1, waiting for transfers between devices, body(): lax.all_gather(scaled_grad, 'tensor', axis=0, tiled=True)  99.5 us
    reduce_scatter x1, waiting for transfers between devices, body(): lax.psum_scatter(lax.dot_general(back_pre, w_in_part, (((1,), (1,)), ((),...  86.1 us
    reduce_scatter x1, waiting for transfers between devices, body(): lax.psum_scatter(grad_in, 'strip', scatter_dimension=0, tiled=True)  61.1 us
    reduce_scatter x1, waiting for transfers between devices, body(): lax.psum_scatter(grad_out, 'strip', scatter_dimension=1, tiled=True)  59.4 us
    all_gather x1, waiting for transfers between devices, body(): lax.all_gather(w_in, 'strip', axis=0, tiled=True)  32.9 us
    all_gather x1, waiting for transfers between devices, body(): lax.all_gather(w_out, 'strip', axis=1, tiled=True)  27.4 us
  transfers between devices with their start and end apart: 11, of which 7 were waited for; matrix products, arithmetic and copies ran while one was open for 7% of the time, Pallas kernels for 0%

commit v1 on v0

--- a/solution.py
+++ b/solution.py
@@ -81,7 +81,10 @@
     )
     normed_all, scaled_all = (
         lax.all_gather(normed_output, "tensor", axis=0, tiled=True),
-        lax.all_gather(scaled_grad, "tensor", axis=0, tiled=True),
+        jnp.concatenate(
+            lax.all_to_all(jnp.stack([scaled_grad] * lax.axis_size("tensor")), "tensor", 0, 0),
+            axis=0,
+        ),
     )
     pre_act = jnp.dot(normed_all, w_in_part, preferred_element_type=jnp.float32) + b_in
     hidden_act = gelu_value(pre_act).astype(jnp.bfloat16)

time: 561 us -> 566 us (level)
  starting transfers between devices: 13.6 us -> 23.5 us
    all_gather x1 -> x0, waiting for transfers between devices: 99.5 us -> none  [body(): lax.all_gather(scaled_grad, 'tensor', axis=0, tiled=True)]
    all_gather x1, waiting for transfers between devices: 100 us -> 168 us  [body(): lax.all_gather(normed_output, 'tensor', axis=0, tiled=True)]
    all_gather x1, waiting for transfers between devices: 32.9 us -> 54.9 us  [body(): lax.all_gather(w_in, 'strip', axis=0, tiled=True)]
    all_to_all x0 -> x1, starting transfers between devices: none -> 11.6 us  [body(): lax.all_to_all(jnp.stack([scaled_grad] * lax.axis_size('tensor')), 'tenso...]
  transfers between devices with their start and end apart: 11 -> 11, of which waited for: 7 -> 6; matrix products, arithmetic and copies ran while one was open for 7% -> 7% of each run, Pallas kernels for 0% -> 0%
where the time goes in v1:
time: 566 us
  waiting for transfers between devices  464 us (82%)
  matrix products  38.4 us (7%)
  starting transfers between devices  23.5 us (4%)
  other arithmetic  19.6 us (3%)
  between operations  14.3 us (3%)
  local copies, waits for them, and re-layouts  6.08 us (1%)
    all_gather x1, waiting for transfers between devices, body(): lax.all_gather(normed_output, 'tensor', axis=0, tiled=True)  168 us
    reduce_scatter x1, waiting for transfers between devices, body(): lax.psum_scatter(lax.dot_general(back_pre, w_in_part, (((1,), (1,)), ((),...  89.5 us
    reduce_scatter x1, waiting for transfers between devices, body(): lax.psum_scatter(grad_in, 'strip', scatter_dimension=0, tiled=True)  63.1 us
    reduce_scatter x1, waiting for transfers between devices, body(): lax.psum_scatter(grad_out, 'strip', scatter_dimension=1, tiled=True)  59.4 us
    all_gather x1, waiting for transfers between devices, body(): lax.all_gather(w_in, 'strip', axis=0, tiled=True)  54.9 us
    all_gather x1, waiting for transfers between devices, body(): lax.all_gather(w_out, 'strip', axis=1, tiled=True)  27.4 us
    all_to_all x1, starting transfers between devices, body(): lax.all_to_all(jnp.stack([scaled_grad] * lax.axis_size('tensor')), 'tenso...  11.6 us
  transfers between devices with their start and end apart: 11, of which 6 were waited for; matrix products, arithmetic and copies ran while one was open for 7% of the time, Pallas kernels for 0%

profile of v1, /device:TPU:2, one launch (start us, length us, event | category | flops | bytes accessed | tf_op | source)
XLA Modules:
  0.0 565.8 jit_solution(8753625035293483209)
XLA Ops:
  7.2 0.0 all-gather.8.cloned.1.call-start
  7.2 0.7 all-gather.8.cloned.1.call-update
  7.9 0.0 all-gather.6.cloned.1.call-start
  7.9 1.1 convert_reduce_fusion
  9.1 0.1 div.16
  9.2 1.2 multiply_reduce_fusion.1
  10.4 0.1 rsqrt.12
  10.5 2.1 add_convert_fusion
  12.6 0.0 all-gather.6.cloned.1.call-update
  12.6 1.1 fusion.59
  13.7 3.3 stack.2
  17.0 11.6 %all-to-all-start = ((bf16[16,128,1536]{2,1,0:T(8,128)(2,1)}), bf16[16,128,1536]{2,1,0:T(8,128)(2,1)}, u32[]{:S(2)}, u32[]{:S(2)}) async-start(bf16[16,128,1536]{2,1,0:T(8,128)(2,1)} %stack.2), calls=%async_computation | async-start | bytes 12582912 | tf_op jit(solution)/shard_map/all_to_all | solution.py:85
  28.6 0.0 all-gather.4.cloned.1.call-start
  28.6 0.7 all-gather.4.cloned.1.call-update
  29.3 0.0 reduce-scatter.4.cloned.1.call-start
  29.3 54.9 %all-gather.8.cloned.1.call-done = bf16[1536,384]{1,0:T(8,128)(2,1)} async-done(((bf16[96,384]{1,0:T(8,128)(2,1)}), bf16[1536,384]{1,0:T(8,128)(2,1)}) %all-gather.8.cloned.1.call-update) | async-done | bytes 1179664 | tf_op jit(solution)/shard_map/all_gather | solution.py:79
  84.2 168.2 %all-gather.6.cloned.1.call-done = bf16[2048,1536]{1,0:T(8,128)(2,1)} async-done(((bf16[128,1536]{1,0:T(8,128)(2,1)}), bf16[2048,1536]{1,0:T(8,128)(2,1)}) %all-gather.6.cloned.1.call-update) | async-done | bytes 6291472 | tf_op jit(solution)/shard_map/all_gather | solution.py:83
  252.5 8.2 %convolution_add_fusion = f32[2048,384]{1,0:T(8,128)} fusion(bf16[2048,1536]{1,0:T(8,128)(2,1)} %all-gather.6.cloned.1.call-done, bf16[1536,384]{1,0:T(8,128)(2,1)} %all-gather.8.cloned.1.call-done, f32[384]{0:T(512)S(1)} %copy-done.5), kind=kOutput, calls=%fused_computation.10 | convolution fusion | flops 2416705536 | bytes 10618368 | tf_op jit(solution)/shard_map/dot_general | solution.py:89
  260.7 27.4 %all-gather.4.cloned.1.call-done = bf16[384,1536]{0,1:T(8,128)(2,1)} async-done(((bf16[384,96]{0,1:T(8,128)(2,1)}), bf16[384,1536]{0,1:T(8,128)(2,1)}) %all-gather.4.cloned.1.call-update) | async-done | bytes 1179664 | tf_op jit(solution)/shard_map/all_gather | solution.py:80
  288.1 8.4 %fusion.5 = bf16[2048,384]{1,0:T(8,128)(2,1)S(1)} fusion(f32[2048,384]{1,0:T(8,128)} %convolution_add_fusion, bf16[2048,1536]{1,0:T(8,128)(2,1)} %bitcast.1, bf16[384,1536]{0,1:T(8,128)(2,1)} %all-gather.4.cloned.1.call-done), kind=kOutput, calls=%fused_computation.7 | convolution fusion | flops 2423783424 | bytes 12189696 | tf_op jit(solution)/shard_map/dot_general | solution.py:91
  296.5 5.4 convolution_convert_fusion
  301.9 0.0 reduce-scatter.4.cloned.1.call-update
  301.9 0.2 reduce-scatter.6.cloned.1.call-start
  302.1 7.7 %fusion.63 = f32[1536,384]{1,0:T(8,128)} fusion(bf16[2048,1536]{1,0:T(8,128)(2,1)} %all-gather.6.cloned.1.call-done, bf16[2048,384]{1,0:T(8,128)(2,1)S(1)} %fusion.5), kind=kOutput, calls=%fused_computation.184 | convolution fusion | flops 2415919104 | bytes 10223616 | tf_op jit(solution)/shard_map/dot_general | solution.py:95
  309.8 0.0 reduce-scatter.6.cloned.1.call-update
  309.9 0.0 copy-start.2
  309.9 0.0 copy-start.3
  309.9 0.0 reduce-scatter.8.cloned.1.call-start
  309.9 8.7 %fusion.6 = f32[384,1536]{0,1:T(8,128)} fusion(bf16[2048,1536]{1,0:T(8,128)(2,1)} %bitcast.1, f32[2048,384]{1,0:T(8,128)} %convolution_add_fusion), kind=kOutput, calls=%fused_computation.11 | convolution fusion | flops 2419851264 | bytes 11796480 | tf_op jit(solution)/shard_map/dot_general | solution.py:98
  318.6 0.0 reduce-scatter.8.cloned.1.call-update
  318.7 0.8 slice_reduce_fusion.46
  319.5 0.9 slice_reduce_fusion.48
  320.4 0.9 slice_reduce_fusion.47
  321.3 89.5 %reduce-scatter.4.cloned.1.call-done = bf16[128,1536]{1,0:T(8,128)(2,1)} async-done(((bf16[2048,1536]{1,0:T(8,128)(2,1)}), bf16[128,1536]{1,0:T(8,128)(2,1)}) %reduce-scatter.4.cloned.1.call-update) | async-done | bytes 393232 | tf_op jit(solution)/shard_map/reduce_scatter | solution.py:101
  410.8 1.3 fusion.60
  412.1 0.0 copy-start.1
  412.1 1.4 multiply_convert_fusion.2
  413.5 1.3 collective-permute-start
  414.8 1.3 collective-permute-start.1
  416.1 63.1 %reduce-scatter.6.cloned.1.call-done = f32[96,384]{1,0:T(8,128)} async-done(((f32[1536,384]{1,0:T(8,128)}), f32[96,384]{1,0:T(8,128)}) %reduce-scatter.6.cloned.1.call-update) | async-done | bytes 147472 | tf_op jit(solution)/shard_map/reduce_scatter | solution.py:110
  479.2 1.6 broadcast_multiply_fusion.1
  480.8 0.1 pad_maximum_fusion.2
  480.9 4.6 collective-permute-start.2
  485.6 4.2 collective-permute-start.3
  489.8 59.4 %reduce-scatter.8.cloned.1.call-done = f32[384,96]{0,1:T(8,128)} async-done(((f32[384,1536]{0,1:T(8,128)}), f32[384,96]{0,1:T(8,128)}) %reduce-scatter.8.cloned.1.call-update) | async-done | bytes 147472 | tf_op jit(solution)/shard_map/reduce_scatter | solution.py:111
  549.3 1.6 broadcast_multiply_fusion
  550.8 0.4 maximum_convert_fusion
  551.2 7.7 %fusion.10 = bf16[8,16,1536]{2,1,0:T(8,128)(2,1)} fusion(f32[14,22,1536]{2,1,0:T(8,128)S(1)} %maximum_convert_fusion, f32[1536]{0:T(1024)} %get-tuple-element.52, f32[1536]{0:T(1024)} %get-tuple-element.53, f32[1536]{0:T(1024)} %get-tuple-element.6, f32[1536]{0:T(1024)} %get-tuple-element.7, f32[1536]{0:T(1024)} %get-tuple-element.8, ...), kind=kLoop, calls=%fused_computation.17 | loop fusion | flops 19660800 | bytes 39622656 | tf_op jit(solution)/shard_map/convert_element_type | solution.py:124
  (18 shorter events, 0.1 us)
Async XLA Ops:
  7.2 77.1 %all-gather.8.cloned.1.call-start = ((), (), s32[]{:S(2)}) async-start(), calls=%async_computation.6 | async-start | bytes 1253376 | tf_op jit(solution)/shard_map/all_gather | solution.py:79
  7.9 244.6 %all-gather.6.cloned.1.call-start = ((), (), s32[]{:S(2)}) async-start(), calls=%async_computation.5 | async-start | bytes 6684672 | tf_op jit(solution)/shard_map/all_gather | solution.py:83
  17.0 235.5 %copy-start.5 = (f32[384]{0:T(512)S(1)}, f32[384]{0:T(512)}, u32[]{:S(2)}) copy-start(f32[384]{0:T(512)} %param.14) | copy-start | bytes 4612
  17.0 271.1 %all-to-all-start = ((bf16[16,128,1536]{2,1,0:T(8,128)(2,1)}), bf16[16,128,1536]{2,1,0:T(8,128)(2,1)}, u32[]{:S(2)}, u32[]{:S(2)}) async-start(bf16[16,128,1536]{2,1,0:T(8,128)(2,1)} %stack.2), calls=%async_computation | async-start | bytes 12582912 | tf_op jit(solution)/shard_map/all_to_all | solution.py:85
  28.6 259.5 %all-gather.4.cloned.1.call-start = ((), (), s32[]{:S(2)}) async-start(), calls=%async_computation.4 | async-start | bytes 1253376 | tf_op jit(solution)/shard_map/all_gather | solution.py:80
  29.3 381.5 %reduce-scatter.4.cloned.1.call-start = ((), (), s32[]{:S(2)}) async-start(), calls=%async_computation.7 | async-start | bytes 6684672 | tf_op jit(solution)/shard_map/reduce_scatter | solution.py:101
  288.1 8.4 %copy-start.4 = (bf16[1536,384]{1,0:T(8,128)(2,1)S(1)}, bf16[1536,384]{1,0:T(8,128)(2,1)}, u32[]{:S(2)}) copy-start(bf16[1536,384]{1,0:T(8,128)(2,1)} %all-gather.8.cloned.1.call-done) | copy-start | bytes 3538948
  301.9 177.3 %reduce-scatter.6.cloned.1.call-start = ((), (), s32[]{:S(2)}) async-start(), calls=%async_computation.8 | async-start | bytes 2506752 | tf_op jit(solution)/shard_map/reduce_scatter | solution.py:110
  309.9 8.8 %copy-start.2 = (f32[7,7,1536]{2,1,0:T(8,128)S(1)}, f32[7,7,1536]{2,1,0:T(8,128)}, u32[]{:S(2)}) copy-start(f32[7,7,1536]{2,1,0:T(8,128)} %param.17) | copy-start | bytes 903172
  309.9 100.9 %copy-start.3 = (f32[1536]{0:T(1024)S(1)}, f32[1536]{0:T(1024)}, u32[]{:S(2)}) copy-start(f32[1536]{0:T(1024)} %param.11) | copy-start | bytes 18436
  309.9 239.4 %reduce-scatter.8.cloned.1.call-start = ((), (), s32[]{:S(2)}) async-start(), calls=%async_computation.9 | async-start | bytes 2506752 | tf_op jit(solution)/shard_map/reduce_scatter | solution.py:111
  318.6 92.2 %copy-start = (bf16[8,16,1536]{2,1,0:T(8,128)(2,1)S(1)}, bf16[8,16,1536]{2,1,0:T(8,128)(2,1)}, u32[]{:S(2)}) copy-start(bf16[8,16,1536]{2,1,0:T(8,128)(2,1)} %param.9) | copy-start | bytes 1179652
  412.1 139.1 %copy-start.1 = (bf16[8,16,1536]{2,1,0:T(8,128)(2,1)S(1)}, bf16[8,16,1536]{2,1,0:T(8,128)(2,1)}, u32[]{:S(2)}) copy-start(bf16[8,16,1536]{2,1,0:T(8,128)(2,1)} %param.10) | copy-start | bytes 1179652
  413.5 67.3 %collective-permute-start = (bf16[3,16,1536]{2,1,0:T(8,128)(2,1)S(1)}, bf16[3,16,1536]{2,1,0:T(8,128)(2,1)S(1)}, u32[]{:S(2)}, u32[]{:S(2)}) collective-permute-start(bf16[3,16,1536]{2,1,0:T(8,128)(2,1)S(1)} %bitcast.30), channel_id=1, source_target_pairs={{0,16},{16,32},{32,48},{48,64},{64,80},{80,96},{96,112},{112,128},... | collective-permute-start | bytes 442376 | tf_op jit(solution)/shard_map/ppermute | solution.py:17
  414.8 66.0 %collective-permute-start.1 = (bf16[3,16,1536]{2,1,0:T(8,128)(2,1)S(1)}, bf16[3,16,1536]{2,1,0:T(8,128)(2,1)S(1)}, u32[]{:S(2)}, u32[]{:S(2)}) collective-permute-start(bf16[3,16,1536]{2,1,0:T(8,128)(2,1)S(1)} %bitcast.29), channel_id=1, source_target_pairs={{16,0},{32,16},{48,32},{64,48},{80,64},{96,80},{112,96},{128,112},... | collective-permute-start | bytes 442376 | tf_op jit(solution)/shard_map/ppermute | solution.py:20
  480.9 69.9 %collective-permute-start.2 = (bf16[14,3,1536]{2,1,0:T(4,128)(2,1)S(1)}, bf16[14,3,1536]{2,1,0:T(4,128)(2,1)S(1)}, u32[]{:S(2)}, u32[]{:S(2)}) collective-permute-start(bf16[14,3,1536]{2,1,0:T(4,128)(2,1)S(1)} %get-tuple-element.54), channel_id=1, source_target_pairs={{0,1},{1,2},{2,3},{3,4},{4,5},{5,6},{6,7},{7,8},{8,9},{9,10},{10,1... | collective-permute-start | bytes 387080 | tf_op jit(solution)/shard_map/ppermute | solution.py:17
  485.6 65.3 %collective-permute-start.3 = (bf16[14,3,1536]{2,1,0:T(4,128)(2,1)S(1)}, bf16[14,3,1536]{2,1,0:T(4,128)(2,1)S(1)}, u32[]{:S(2)}, u32[]{:S(2)}) collective-permute-start(bf16[14,3,1536]{2,1,0:T(4,128)(2,1)S(1)} %get-tuple-element.55), channel_id=1, source_target_pairs={{1,0},{2,1},{3,2},{4,3},{5,4},{6,5},{7,6},{8,7},{9,8},{10,9},{11,1... | collective-permute-start | bytes 387080 | tf_op jit(solution)/shard_map/ppermute | solution.py:20
Sparse Core Ops, SparseCore 0:
  9.8 74.3 all-gather.7
  87.3 165.1 all-gather.5
  254.3 33.7 all-gather.3
  302.0 108.7 reduce-scatter.3
  413.2 65.9 reduce-scatter.5
  481.6 67.6 reduce-scatter.7
